TPU v7x, 32 devices: a whole 2x2x4 slice. The times are simulated.
32 devices in a mesh: band: 4 (over y, core), grid: 8 (over z, x).
Axes of the slice: x: 2, y: 2, z: 4, core: 2. Of those that a mesh axis runs over, the one named last changes fastest.
Arguments:
- orbitals: float32 [64, 16, 4096], P('band', 'grid'), may hold values from -6 to 6
- potential: float32 [16, 4096], P('grid'), may hold values from 0 to 2
Outputs:
- rotated: bfloat16 [64, 16, 4096], P('band', 'grid')
All inputs are finite; a program needn't handle non-finite values. Where the computation divides by a largest or mean magnitude, that divisor is 1e-20 or more.
Results may differ from a plain program's by a relative error of at most 0.001.
The roundings to bfloat16 on the way count: a program that leaves them out, or rounds other values in their place, can miss the bound.
Values may be sent and summed in bfloat16 or wider, within the bound.
A program may use at most 64 MiB of HBM per device.

v0:
```python
import jax
import jax.numpy as jnp
from jax import lax
from jax.sharding import PartitionSpec as P

NX = 64
DEGREE = 2
NS_ITERS = 2


def with_halo(block, sides, width):
    for axis, dim in sides:
        count = lax.axis_size(axis)
        forward = [(i, i + 1) for i in range(count - 1)]
        forward.append((count - 1, 0))
        backward = [(target, source) for source, target in forward]
        low = lax.ppermute(
            lax.slice_in_dim(block, block.shape[dim] - width, None, axis=dim), axis, forward
        )
        high = lax.ppermute(lax.slice_in_dim(block, 0, width, axis=dim), axis, backward)
        block = jnp.concatenate([low, block, high], axis=dim)
    return block


def apply_inner(extended, potential):
    inner = extended[:, 1:-1]
    count = inner.shape[0]
    planes = inner.shape[1]
    square = inner.reshape(count, planes, NX, NX)
    sideways = jnp.roll(square, 1, 2) + jnp.roll(square, -1, 2)
    sideways = sideways + jnp.roll(square, 1, 3) + jnp.roll(square, -1, 3)
    beside = extended[:, 2:] + extended[:, :-2] + sideways.reshape(inner.shape)
    return 0.5 * (6.0 * inner - beside) + potential[None] * inner


def local(orbitals, potential):
    previous = orbitals
    current = orbitals
    for degree_step in range(DEGREE):
        extended = with_halo(current, (("grid", 1),), 1)
        applied = apply_inner(extended, potential)
        if degree_step == 0:
            following = (applied - 5.0 * current) / 3.0
        else:
            following = 2.0 * (applied - 5.0 * current) / 3.0 - previous
        previous = current
        current = following
    count, zplanes, width = orbitals.shape
    filtered = current.astype(jnp.bfloat16).reshape(count, zplanes * width)
    pieces = lax.all_to_all(filtered, "band", split_axis=1, concat_axis=0, tiled=True)
    total_cells = pieces.shape[1] * lax.axis_size("band") * lax.axis_size("grid")
    partial_value = (
        lax.dot_general(
            pieces, pieces, (((1,), (1,)), ((), ())), preferred_element_type=jnp.float32
        )
        / total_cells
    )
    gram = lax.psum(partial_value, ("band", "grid"))
    scale = jnp.max(jnp.sum(jnp.abs(gram), axis=1))
    identity_mat = jnp.eye(gram.shape[0], dtype=jnp.float32)
    upper = gram / scale
    lower = identity_mat
    for sweep in range(NS_ITERS):
        factor = 1.5 * identity_mat - 0.5 * jnp.dot(lower, upper, precision=lax.Precision.HIGHEST)
        upper = jnp.dot(upper, factor, precision=lax.Precision.HIGHEST)
        lower = jnp.dot(factor, lower, precision=lax.Precision.HIGHEST)
    root = (lower / jnp.sqrt(scale)).astype(jnp.bfloat16)
    turned = lax.dot_general(
        root, pieces, (((0,), (0,)), ((), ())), preferred_element_type=jnp.float32
    )
    turned = turned.astype(jnp.bfloat16)
    returned = lax.all_to_all(turned, "band", split_axis=0, concat_axis=1, tiled=True)
    return returned.reshape(count, zplanes, width)


def solution(mesh):
    placed = (P("band", "grid", None), P("grid", None))
    return jax.shard_map(
        local, mesh=mesh, in_specs=placed, out_specs=P("band", "grid", None), check_vma=False
    )
```

profile of v0, /device:TPU:1, one launch (start us, length us, event | category | flops | bytes accessed | tf_op | source)
XLA Modules:
  0.0 101.3 jit_solution(3121627851999156750)
XLA Ops:
  0.0 1.9 %fusion.24 = (f32[16,1,4096]{2,1,0:T(1,128)S(1)}, f32[16,1,4096]{2,1,0:T(1,128)S(1)}) fusion(f32[16,2,4096]{2,1,0:T(2,128)} %param.2), kind=kLoop, calls=%fused_computation.42 | loop fusion | bytes 1048576 | tf_op jit(solution)/shard_map/slice | solution.py:20
  1.9 5.1 %collective-permute-start = (f32[16,1,4096]{2,1,0:T(1,128)S(1)}, f32[16,1,4096]{2,1,0:T(1,128)S(1)}, u32[]{:S(2)}, u32[]{:S(2)}) collective-permute-start(f32[16,1,4096]{2,1,0:T(1,128)S(1)} %get-tuple-element.25), channel_id=1, source_target_pairs={{1,0},{2,1},{3,2},{4,3},{5,4},{6,5},{7,6},{0,7},{9,8},{10,9},{11,1... | collective-permute-start | bytes 786440 | tf_op jit(solution)/shard_map/ppermute | solution.py:20
  7.0 0.6 reshape.35
  7.6 0.4 fusion.19
  8.0 0.4 fusion.20
  8.6 0.5 copy-done.1
  9.2 0.9 fusion.4
  10.1 0.5 add.58
  10.6 1.4 %collective-permute-done = f32[16,1,4096]{2,1,0:T(1,128)S(1)} collective-permute-done((f32[16,1,4096]{2,1,0:T(1,128)S(1)}, f32[16,1,4096]{2,1,0:T(1,128)S(1)}, u32[]{:S(2)}, u32[]{:S(2)}) %collective-permute-start) | collective-permute-done | bytes 262176 | tf_op jit(solution)/shard_map/ppermute | solution.py:20
  12.0 4.7 %collective-permute-done.1 = f32[16,1,4096]{2,1,0:T(1,128)} collective-permute-done((f32[16,1,4096]{2,1,0:T(1,128)S(1)}, f32[16,1,4096]{2,1,0:T(1,128)}, u32[]{:S(2)}, u32[]{:S(2)}) %collective-permute-start.1) | collective-permute-done | bytes 262176 | tf_op jit(solution)/shard_map/ppermute | solution.py:17
  16.7 2.4 %broadcast_multiply_fusion = (f32[16,2,4096]{2,1,0:T(2,128)S(1)}, f32[16,2,4096]{2,1,0:T(2,128)S(1)}) fusion(f32[16,2,4096]{2,1,0:T(2,128)S(1)} %copy-done, f32[2,4096]{1,0:T(2,128)S(1)} %copy-done.1, f32[16,2,4096]{2,1,0:T(2,128)S(1)} %add.58, f32[16,1,4096]{2,1,0:T(1,128)} %collective-permute-done.1, f32[16,1,4096]{2,1,0:T(1,128)S(1)} %collective-permute-done), kind=kLoop, calls=%fused_computation.26 | loop fusion | flops 1572864 | bytes 2654208 | tf_op jit(solution)/shard_map/div | solution.py:43
  19.2 0.6 reshape.36
  19.8 0.4 fusion.16
  20.2 0.2 fusion.17
  20.4 0.4 fusion.15
  20.7 1.3 %fusion.23 = (f32[16,1,4096]{2,1,0:T(1,128)}, f32[16,1,4096]{2,1,0:T(1,128)}) fusion(f32[16,2,4096]{2,1,0:T(2,128)S(1)} %get-tuple-element.5), kind=kLoop, calls=%fused_computation.41 | loop fusion | bytes 1048576 | tf_op jit(solution)/shard_map/slice | solution.py:20
  22.1 3.2 %collective-permute-start.2 = (f32[16,1,4096]{2,1,0:T(1,128)}, f32[16,1,4096]{2,1,0:T(1,128)S(1)}, u32[]{:S(2)}, u32[]{:S(2)}) collective-permute-start(f32[16,1,4096]{2,1,0:T(1,128)} %get-tuple-element.23), channel_id=1, source_target_pairs={{1,0},{2,1},{3,2},{4,3},{5,4},{6,5},{7,6},{0,7},{9,8},{10,9},{11,1... | collective-permute-start | bytes 786440 | tf_op jit(solution)/shard_map/ppermute | solution.py:20
  25.3 0.9 fusion.6
  26.2 0.5 add.65
  26.7 2.9 %collective-permute-done.2 = f32[16,1,4096]{2,1,0:T(1,128)S(1)} collective-permute-done((f32[16,1,4096]{2,1,0:T(1,128)}, f32[16,1,4096]{2,1,0:T(1,128)S(1)}, u32[]{:S(2)}, u32[]{:S(2)}) %collective-permute-start.2) | collective-permute-done | bytes 262176 | tf_op jit(solution)/shard_map/ppermute | solution.py:20
  29.6 7.4 %collective-permute-done.3 = f32[16,1,4096]{2,1,0:T(1,128)} collective-permute-done((f32[16,1,4096]{2,1,0:T(1,128)}, f32[16,1,4096]{2,1,0:T(1,128)}, u32[]{:S(2)}, u32[]{:S(2)}) %collective-permute-start.3) | collective-permute-done | bytes 262176 | tf_op jit(solution)/shard_map/ppermute | solution.py:17
  37.0 2.6 %subtract_convert_fusion = bf16[16,2,4096]{2,1,0:T(2,128)(2,1)S(1)} fusion(f32[16,2,4096]{2,1,0:T(2,128)S(1)} %copy-done, f32[16,2,4096]{2,1,0:T(2,128)S(1)} %get-tuple-element.6, f32[16,2,4096]{2,1,0:T(2,128)S(1)} %add.65, f32[16,2,4096]{2,1,0:T(2,128)S(1)} %get-tuple-element.5, f32[16,1,4096]{2,1,0:T(1,128)} %collective-permute-done.3, ...), kind=kLoop, calls=%fused_computation.24 | loop fusion | flops 1835008 | bytes 2916352 | tf_op jit(solution)/shard_map/convert_element_type | solution.py:49
  39.8 8.0 %all_to_all.35 = bf16[16,4,2048]{2,0,1:T(8,128)(2,1)S(1)} all-to-all(bf16[16,4,2048]{2,0,1:T(8,128)(2,1)S(1)} %copy.7), channel_id=1, replica_groups=mesh['band'=4,'grid'=8] {'band'}, dimensions={1} | all-to-all | bytes 524288 | tf_op jit(solution)/shard_map/all_to_all | solution.py:50
  47.9 0.2 convolution_multiply_fusion.2
  48.1 38.6 %psum.7 = f32[64,64]{1,0:T(8,128)S(1)} all-reduce(f32[64,64]{1,0:T(8,128)S(1)} %convolution_multiply_fusion.2), channel_id=1, replica_groups=mesh['band'=4,'grid'=8] {'band','grid'}, use_global_device_ids=true, to_apply=%region_0.1 | all-reduce | flops 4096 | bytes 32768 | tf_op jit(solution)/shard_map/psum | solution.py:58
  86.8 0.6 reduce_max.9
  87.4 0.8 fusion.1
  88.2 0.8 fusion.14
  90.2 0.2 convolution_convert_fusion
  90.5 9.8 %all_to_all.36 = bf16[4,16,2048]{2,1,0:T(8,128)(2,1)S(1)} all-to-all(bf16[4,16,2048]{2,1,0:T(8,128)(2,1)S(1)} %bitcast.21), channel_id=1, replica_groups=mesh['band'=4,'grid'=8] {'band'}, dimensions={0} | all-to-all | bytes 524288 | tf_op jit(solution)/shard_map/all_to_all | solution.py:72
  100.2 0.2 copy.8
  100.4 0.9 reshape.37
  (15 shorter events, 1.1 us)
Async XLA Ops:
  0.0 7.0 %copy-start = (f32[16,2,4096]{2,1,0:T(2,128)S(1)}, f32[16,2,4096]{2,1,0:T(2,128)}, u32[]{:S(2)}) copy-start(f32[16,2,4096]{2,1,0:T(2,128)} %param.2) | copy-start | bytes 1572868
  1.9 10.1 %collective-permute-start = (f32[16,1,4096]{2,1,0:T(1,128)S(1)}, f32[16,1,4096]{2,1,0:T(1,128)S(1)}, u32[]{:S(2)}, u32[]{:S(2)}) collective-permute-start(f32[16,1,4096]{2,1,0:T(1,128)S(1)} %get-tuple-element.25), channel_id=1, source_target_pairs={{1,0},{2,1},{3,2},{4,3},{5,4},{6,5},{7,6},{0,7},{9,8},{10,9},{11,1... | collective-permute-start | bytes 786440 | tf_op jit(solution)/shard_map/ppermute | solution.py:20
  7.0 9.7 %collective-permute-start.1 = (f32[16,1,4096]{2,1,0:T(1,128)S(1)}, f32[16,1,4096]{2,1,0:T(1,128)}, u32[]{:S(2)}, u32[]{:S(2)}) collective-permute-start(f32[16,1,4096]{2,1,0:T(1,128)S(1)} %get-tuple-element.26), channel_id=1, source_target_pairs={{0,1},{1,2},{2,3},{3,4},{4,5},{5,6},{6,7},{7,0},{8,9},{9,10},{10,1... | collective-permute-start | bytes 786440 | tf_op jit(solution)/shard_map/ppermute | solution.py:17
  8.4 0.8 copy-start.1
  22.1 7.5 %collective-permute-start.2 = (f32[16,1,4096]{2,1,0:T(1,128)}, f32[16,1,4096]{2,1,0:T(1,128)S(1)}, u32[]{:S(2)}, u32[]{:S(2)}) collective-permute-start(f32[16,1,4096]{2,1,0:T(1,128)} %get-tuple-element.23), channel_id=1, source_target_pairs={{1,0},{2,1},{3,2},{4,3},{5,4},{6,5},{7,6},{0,7},{9,8},{10,9},{11,1... | collective-permute-start | bytes 786440 | tf_op jit(solution)/shard_map/ppermute | solution.py:20
  25.3 11.8 %collective-permute-start.3 = (f32[16,1,4096]{2,1,0:T(1,128)}, f32[16,1,4096]{2,1,0:T(1,128)}, u32[]{:S(2)}, u32[]{:S(2)}) collective-permute-start(f32[16,1,4096]{2,1,0:T(1,128)} %get-tuple-element.24), channel_id=1, source_target_pairs={{0,1},{1,2},{2,3},{3,4},{4,5},{5,6},{6,7},{7,0},{8,9},{9,10},{10,1... | collective-permute-start | bytes 786440 | tf_op jit(solution)/shard_map/ppermute | solution.py:17
where the time goes:
time: 103 us; the launch traced here: 101 us
  blocking collectives  56.4 us (55%)
  waiting for transfers between devices  16.5 us (16%)
  local copies, waits for them, and re-layouts  9.32 us (9%)
  starting transfers between devices  8.3 us (8%)
  other arithmetic  7.48 us (7%)
  matrix products  2.54 us (2%)
    psum x1, blocking collectives, local(): gram = lax.psum(partial_value, ('band', 'grid'))  38.6 us
    ppermute x2, waiting for transfers between devices, with_halo(): lax.ppermute(lax.slice_in_dim(block, block.shape[dim] - width, None, axis...  12.1 us
    all_to_all x1, blocking collectives, local(): lax.all_to_all(turned, 'band', split_axis=0, concat_axis=1, tiled=True)  9.75 us
    ppermute x2, starting transfers between devices, with_halo(): lax.ppermute(lax.slice_in_dim(block, 0, width, axis=dim), axis, backward)  8.29 us
    all_to_all x1, blocking collectives, local(): lax.all_to_all(filtered, 'band', split_axis=1, concat_axis=0, tiled=True)  8.05 us
    ppermute x2, waiting for transfers between devices, with_halo(): lax.ppermute(lax.slice_in_dim(block, 0, width, axis=dim), axis, backward)  4.32 us
    slice x2, local copies, waits for them, and re-layouts, with_halo(): lax.slice_in_dim(block, 0, width, axis=dim)  3.21 us
    convert_element_type x1, other arithmetic, local(): filtered = current.astype(jnp.bfloat16).reshape(count, zplanes * width)  2.58 us
  transfers between devices with their start and end apart: 4, of which 4 were waited for; matrix products, arithmetic and copies ran while one was open for 4% of the time, Pallas kernels for 0%

commit v1 on v0

v1 whole, which is shorter than its diff:
```python
import functools

import jax
import jax.numpy as jnp
from jax import lax
from jax.experimental import pallas as pl
from jax.experimental.pallas import tpu as pltpu
from jax.sharding import PartitionSpec as P

NX = 64
DEGREE = 2
NS_ITERS = 2


def with_halo(block, sides, width):
    for axis, dim in sides:
        count = lax.axis_size(axis)
        forward = [(i, i + 1) for i in range(count - 1)]
        forward.append((count - 1, 0))
        backward = [(target, source) for source, target in forward]
        low = lax.ppermute(
            lax.slice_in_dim(block, block.shape[dim] - width, None, axis=dim), axis, forward
        )
        high = lax.ppermute(lax.slice_in_dim(block, 0, width, axis=dim), axis, backward)
        block = jnp.concatenate([low, block, high], axis=dim)
    return block


def apply_inner(extended, potential):
    inner = extended[:, 1:-1]
    count = inner.shape[0]
    planes = inner.shape[1]
    square = inner.reshape(count, planes, NX, NX)
    sideways = jnp.roll(square, 1, 2) + jnp.roll(square, -1, 2)
    sideways = sideways + jnp.roll(square, 1, 3) + jnp.roll(square, -1, 3)
    beside = extended[:, 2:] + extended[:, :-2] + sideways.reshape(inner.shape)
    return 0.5 * (6.0 * inner - beside) + potential[None] * inner


def remote(src, dst, send, recv, **where):
    return pltpu.make_async_remote_copy(
        src_ref=src, dst_ref=dst, send_sem=send, recv_sem=recv,
        device_id=where, device_id_type=pl.DeviceIdType.MESH,
    )


def newton_schulz(gram):
    size = gram.shape[0]
    scale = jnp.max(jnp.sum(jnp.abs(gram), axis=1, keepdims=True), axis=0, keepdims=True)
    rows = lax.broadcasted_iota(jnp.int32, (size, size), 0)
    cols = lax.broadcasted_iota(jnp.int32, (size, size), 1)
    identity_mat = (rows == cols).astype(jnp.float32)
    upper = gram / scale
    lower = None
    for sweep in range(NS_ITERS):
        product = upper if lower is None else jnp.dot(
            lower, upper, precision=lax.Precision.HIGHEST, preferred_element_type=jnp.float32)
        factor = 1.5 * identity_mat - 0.5 * product
        if sweep < NS_ITERS - 1:
            upper = jnp.dot(upper, factor, precision=lax.Precision.HIGHEST,
                            preferred_element_type=jnp.float32)
        lower = factor if lower is None else jnp.dot(
            factor, lower, precision=lax.Precision.HIGHEST, preferred_element_type=jnp.float32)
    return lower / jnp.sqrt(scale)


def exchange(n, axis, me, src_of, dst_of, send, recv):
    sends = []
    for step in range(1, n):
        peer = lax.rem(me + step, n)
        copy = remote(src_of(peer), dst_of(me), send.at[step], recv.at[step], **{axis: peer})
        copy.start()
        sends.append(copy)

    def arrived():
        for step in range(1, n):
            source = lax.rem(me + n - step, n)
            remote(src_of(source), dst_of(source), send.at[step], recv.at[step],
                   **{axis: source}).wait_recv()

    def sent():
        for copy in sends:
            copy.wait_send()

    return arrived, sent


def rows_of(index, size):
    return pl.ds(pl.multiple_of(index * size, size), size)


def tail(nb, ng, count, filt_ref, out_ref, pieces, turned, gpart, rs, gr, gfull,
         own_sem, s0, r0, s1, r1, s2, r2, s3, r3, s4, r4):
    orbs = nb * count
    share = pieces.shape[1]
    total_cells = share * nb * ng
    b = lax.axis_index("band")
    g = lax.axis_index("grid")
    own = pltpu.make_async_copy(
        filt_ref.at[:, rows_of(b, share)], pieces.at[rows_of(b, count)], own_sem.at[0])
    own.start()
    arrived, sent = exchange(
        nb, "band", b, lambda p: filt_ref.at[:, rows_of(p, share)],
        lambda p: pieces.at[rows_of(p, count)], s0, r0)
    gpart[...] = jnp.zeros_like(gpart)
    own.wait()
    arrived()
    everything = pieces[...]
    gpart[:, :orbs] = lax.dot_general(
        everything, everything, (((1,), (1,)), ((), ())),
        preferred_element_type=jnp.float32) / total_cells
    arrived1, sent1 = exchange(
        nb, "band", b, lambda p: gpart.at[rows_of(p, count)], lambda p: rs.at[p], s1, r1)
    rs[b] = gpart[rows_of(b, count), :]
    arrived1()
    gr[g] = jnp.sum(rs[...], axis=0)
    arrived2, sent2 = exchange(ng, "grid", g, lambda p: gr.at[g], lambda p: gr.at[p], s2, r2)
    arrived2()
    gfull[rows_of(b, count), :] = jnp.sum(gr[...], axis=0)
    arrived3, sent3 = exchange(
        nb, "band", b, lambda p: gfull.at[rows_of(b, count)],
        lambda p: gfull.at[rows_of(p, count)], s3, r3)
    arrived3()
    root = newton_schulz(gfull[:, :orbs]).astype(jnp.bfloat16)
    turned[...] = lax.dot_general(
        root, pieces[...], (((0,), (0,)), ((), ())),
        preferred_element_type=jnp.float32).astype(jnp.bfloat16)
    back = pltpu.make_async_copy(
        turned.at[rows_of(b, count)], out_ref.at[:, rows_of(b, share)], own_sem.at[1])
    back.start()
    arrived4, sent4 = exchange(
        nb, "band", b, lambda p: turned.at[rows_of(p, count)],
        lambda p: out_ref.at[:, rows_of(p, share)], s4, r4)
    arrived4()
    back.wait()
    for done in (sent, sent1, sent2, sent3, sent4):
        done()


def greet(nb, ng):
    b = lax.axis_index("band")
    g = lax.axis_index("grid")
    barrier = pltpu.get_barrier_semaphore()
    for step in range(1, nb):
        pl.semaphore_signal(barrier, inc=1, device_id={"band": lax.rem(b + step, nb)},
                            device_id_type=pl.DeviceIdType.MESH)
    for step in range(1, ng):
        pl.semaphore_signal(barrier, inc=1, device_id={"grid": lax.rem(g + step, ng)},
                            device_id_type=pl.DeviceIdType.MESH)
    pl.semaphore_wait(barrier, nb + ng - 2)


def kernel(nb, ng, count, filt_ref, out_ref, *rest):
    greet(nb, ng)
    tail(nb, ng, count, filt_ref, out_ref, *rest)


def tail_scratch(nb, ng, count, cells):
    orbs = nb * count
    wide = max(128, orbs)
    share = cells // nb
    return [
        pltpu.VMEM((orbs, share), jnp.bfloat16),
        pltpu.VMEM((orbs, share), jnp.bfloat16),
        pltpu.VMEM((orbs, wide), jnp.float32),
        pltpu.VMEM((nb, count, wide), jnp.float32),
        pltpu.VMEM((ng, count, wide), jnp.float32),
        pltpu.VMEM((orbs, wide), jnp.float32),
        pltpu.SemaphoreType.DMA((2,)),
        pltpu.SemaphoreType.DMA((nb,)), pltpu.SemaphoreType.DMA((nb,)),
        pltpu.SemaphoreType.DMA((nb,)), pltpu.SemaphoreType.DMA((nb,)),
        pltpu.SemaphoreType.DMA((ng,)), pltpu.SemaphoreType.DMA((ng,)),
        pltpu.SemaphoreType.DMA((nb,)), pltpu.SemaphoreType.DMA((nb,)),
        pltpu.SemaphoreType.DMA((nb,)), pltpu.SemaphoreType.DMA((nb,)),
    ]


def local(orbitals, potential):
    previous = orbitals
    current = orbitals
    for degree_step in range(DEGREE):
        extended = with_halo(current, (("grid", 1),), 1)
        applied = apply_inner(extended, potential)
        if degree_step == 0:
            following = (applied - 5.0 * current) / 3.0
        else:
            following = 2.0 * (applied - 5.0 * current) / 3.0 - previous
        previous = current
        current = following
    count, zplanes, width = orbitals.shape
    cells = zplanes * width
    nb = lax.axis_size("band")
    ng = lax.axis_size("grid")
    filtered = current.astype(jnp.bfloat16).reshape(count, cells)
    returned = pl.pallas_call(
        functools.partial(kernel, nb, ng, count),
        out_shape=jax.ShapeDtypeStruct((count, cells), jnp.bfloat16),
        in_specs=[pl.BlockSpec(memory_space=pltpu.VMEM)],
        out_specs=pl.BlockSpec(memory_space=pltpu.VMEM),
        scratch_shapes=tail_scratch(nb, ng, count, cells),
        compiler_params=pltpu.CompilerParams(collective_id=0, has_side_effects=True),
    )(filtered)
    return returned.reshape(count, zplanes, width)


def solution(mesh):
    placed = (P("band", "grid", None), P("grid", None))
    return jax.shard_map(
        local, mesh=mesh, in_specs=placed, out_specs=P("band", "grid", None), check_vma=False
    )
```

time: 103 us -> 65.8 us (0.64); the launches traced: 101 us -> 65.6 us
  blocking collectives: 56.4 us -> 0 us
  Pallas kernels: 0 us -> 24.3 us
  matrix products: 2.54 us -> 0 us
  other arithmetic: 7.48 us -> 5.81 us
  local copies, waits for them, and re-layouts: 9.32 us -> 10.7 us
    psum x1 -> x0, blocking collectives: 38.6 us -> none  [local(): gram = lax.psum(partial_value, ('band', 'grid'))]
    pallas_call x0 -> x1, Pallas kernels: none -> 24.3 us  [local(): pl.pallas_call(functools.partial(kernel, nb, ng, count), out_shape=jax.Sh...]
    all_to_all x2 -> x0, blocking collectives: 17.8 us -> none  [the longest x1 9.75 us: local(): lax.all_to_all(turned, 'band', split_axis=0, concat_axis=1, tiled=True)]
    dot_general x7 -> x0, matrix products: 2.54 us -> none  [the longest x2 0.96 us: local(): jnp.dot(lower, upper, precision=lax.Precision.HIGHEST)]
  transfers between devices with their start and end apart: 4 -> 4, of which waited for: 4 -> 4; matrix products, arithmetic and copies ran while one was open for 4% -> 7% of each run, Pallas kernels for 0% -> 0%
where the time goes in v1:
time: 65.8 us; the launch traced here: 65.6 us
  Pallas kernels  24.3 us (37%)
  waiting for transfers between devices  16.4 us (25%)
  local copies, waits for them, and re-layouts  10.7 us (16%)
  starting transfers between devices  8.3 us (13%)
  other arithmetic  5.81 us (9%)
    pallas_call x1, Pallas kernels, local(): pl.pallas_call(functools.partial(kernel, nb, ng, count), out_shape=jax.Sh...  24.3 us
    ppermute x2, waiting for transfers between devices, with_halo(): lax.ppermute(lax.slice_in_dim(block, block.shape[dim] - width, None, axis...  12 us
    ppermute x2, starting transfers between devices, with_halo(): lax.ppermute(lax.slice_in_dim(block, 0, width, axis=dim), axis, backward)  8.29 us
    ppermute x2, waiting for transfers between devices, with_halo(): lax.ppermute(lax.slice_in_dim(block, 0, width, axis=dim), axis, backward)  4.32 us
    slice x2, local copies, waits for them, and re-layouts, with_halo(): lax.slice_in_dim(block, 0, width, axis=dim)  3.22 us
    convert_element_type x1, other arithmetic, local(): filtered = current.astype(jnp.bfloat16).reshape(count, cells)  2.58 us
    reshape x1, local copies, waits for them, and re-layouts, local(): return returned.reshape(count, zplanes, width)  1.85 us
    add x2, other arithmetic, apply_inner(): sideways = sideways + jnp.roll(square, 1, 3) + jnp.roll(square, -1, 3)  1.72 us
  transfers between devices with their start and end apart: 4, of which 4 were waited for; matrix products, arithmetic and copies ran while one was open for 7% of the time, Pallas kernels for 0%

profile of v1, /device:TPU:1, one launch (start us, length us, event | category | flops | bytes accessed | tf_op | source)
XLA Modules:
  0.0 65.6 jit_solution(10302367611724181206)
XLA Ops:
  0.0 0.0 copy-start
  0.0 1.9 %fusion.19 = (f32[16,1,4096]{2,1,0:T(1,128)S(1)}, f32[16,1,4096]{2,1,0:T(1,128)S(1)}) fusion(f32[16,2,4096]{2,1,0:T(2,128)} %param.2), kind=kLoop, calls=%fused_computation.29 | loop fusion | bytes 1048576 | tf_op jit(solution)/shard_map/slice | solution.py:24
  1.9 5.1 %collective-permute-start = (f32[16,1,4096]{2,1,0:T(1,128)S(1)}, f32[16,1,4096]{2,1,0:T(1,128)S(1)}, u32[]{:S(2)}, u32[]{:S(2)}) collective-permute-start(f32[16,1,4096]{2,1,0:T(1,128)S(1)} %get-tuple-element.25), channel_id=1, source_target_pairs={{1,0},{2,1},{3,2},{4,3},{5,4},{6,5},{7,6},{0,7},{9,8},{10,9},{11,1... | collective-permute-start | bytes 786440 | tf_op jit(solution)/shard_map/ppermute | solution.py:24
  7.0 0.0 collective-permute-start.1
  7.0 0.0 copy-done
  7.0 0.6 reshape.29
  7.6 0.4 fusion.14
  8.0 0.4 fusion.15
  8.4 0.0 copy-start.1
  8.4 0.2 fusion.16
  8.6 0.5 copy-done.1
  9.2 0.9 %fusion.1 = f32[16,2,64,64]{3,2,1,0:T(8,128)S(1)} fusion(f32[16,2,63,64]{3,2,1,0:T(8,128)S(1)} %get-tuple-element.20, f32[16,2,1,64]{3,2,1,0:T(1,128)S(1)} %get-tuple-element.22, f32[16,2,1,64]{3,2,1,0:T(1,128)S(1)} %get-tuple-element.21, f32[16,2,63,64]{3,2,1,0:T(8,128)S(1)} %get-tuple-element.19, f32[16,2,64,63]{3,2,1,0:T(8,128)S(1)} %get-tuple-element.16, ...), kind=kLoop, calls=%fused_computation.2 | loop fusion | flops 917504 | bytes 2621440 | tf_op jit(solution)/shard_map/add | solution.py:35
  10.1 0.5 add.56
  10.6 1.4 %collective-permute-done = f32[16,1,4096]{2,1,0:T(1,128)S(1)} collective-permute-done((f32[16,1,4096]{2,1,0:T(1,128)S(1)}, f32[16,1,4096]{2,1,0:T(1,128)S(1)}, u32[]{:S(2)}, u32[]{:S(2)}) %collective-permute-start) | collective-permute-done | bytes 262176 | tf_op jit(solution)/shard_map/ppermute | solution.py:24
  12.0 4.6 %collective-permute-done.1 = f32[16,1,4096]{2,1,0:T(1,128)S(1)} collective-permute-done((f32[16,1,4096]{2,1,0:T(1,128)S(1)}, f32[16,1,4096]{2,1,0:T(1,128)S(1)}, u32[]{:S(2)}, u32[]{:S(2)}) %collective-permute-start.1) | collective-permute-done | bytes 262176 | tf_op jit(solution)/shard_map/ppermute | solution.py:21
  16.6 1.5 %broadcast_multiply_fusion = (f32[16,2,4096]{2,1,0:T(2,128)S(1)}, f32[16,2,4096]{2,1,0:T(2,128)S(1)}) fusion(f32[16,2,4096]{2,1,0:T(2,128)S(1)} %copy-done, f32[2,4096]{1,0:T(2,128)S(1)} %copy-done.1, f32[16,2,4096]{2,1,0:T(2,128)S(1)} %add.56, f32[16,1,4096]{2,1,0:T(1,128)S(1)} %collective-permute-done.1, f32[16,1,4096]{2,1,0:T(1,128)S(1)} %collective-permute-done), kind=kLoop, calls=%fused_computation.18 | loop fusion | flops 1572864 | bytes 2654208 | tf_op jit(solution)/shard_map/div | solution.py:185
  18.1 0.6 reshape.30
  18.7 0.4 fusion.11
  19.1 0.2 fusion.12
  19.3 0.4 fusion.10
  19.7 1.3 %fusion.18 = (f32[16,1,4096]{2,1,0:T(1,128)}, f32[16,1,4096]{2,1,0:T(1,128)}) fusion(f32[16,2,4096]{2,1,0:T(2,128)S(1)} %get-tuple-element.5), kind=kLoop, calls=%fused_computation.28 | loop fusion | bytes 1048576 | tf_op jit(solution)/shard_map/slice | solution.py:24
  21.0 3.2 %collective-permute-start.2 = (f32[16,1,4096]{2,1,0:T(1,128)}, f32[16,1,4096]{2,1,0:T(1,128)S(1)}, u32[]{:S(2)}, u32[]{:S(2)}) collective-permute-start(f32[16,1,4096]{2,1,0:T(1,128)} %get-tuple-element.23), channel_id=1, source_target_pairs={{1,0},{2,1},{3,2},{4,3},{5,4},{6,5},{7,6},{0,7},{9,8},{10,9},{11,1... | collective-permute-start | bytes 786440 | tf_op jit(solution)/shard_map/ppermute | solution.py:24
  24.2 0.0 collective-permute-start.3
  24.2 0.9 %fusion.3 = f32[16,2,64,64]{3,2,1,0:T(8,128)S(1)} fusion(f32[16,2,63,64]{3,2,1,0:T(8,128)S(1)} %get-tuple-element.12, f32[16,2,1,64]{3,2,1,0:T(1,128)S(1)} %get-tuple-element.14, f32[16,2,1,64]{3,2,1,0:T(1,128)S(1)} %get-tuple-element.13, f32[16,2,63,64]{3,2,1,0:T(8,128)S(1)} %get-tuple-element.11, f32[16,2,64,63]{3,2,1,0:T(8,128)S(1)} %get-tuple-element.8, ...), kind=kLoop, calls=%fused_computation.5 | loop fusion | flops 917504 | bytes 2621440 | tf_op jit(solution)/shard_map/add | solution.py:35
  25.1 0.5 add.63
  25.6 2.9 %collective-permute-done.2 = f32[16,1,4096]{2,1,0:T(1,128)S(1)} collective-permute-done((f32[16,1,4096]{2,1,0:T(1,128)}, f32[16,1,4096]{2,1,0:T(1,128)S(1)}, u32[]{:S(2)}, u32[]{:S(2)}) %collective-permute-start.2) | collective-permute-done | bytes 262176 | tf_op jit(solution)/shard_map/ppermute | solution.py:24
  28.6 7.4 %collective-permute-done.3 = f32[16,1,4096]{2,1,0:T(1,128)} collective-permute-done((f32[16,1,4096]{2,1,0:T(1,128)}, f32[16,1,4096]{2,1,0:T(1,128)}, u32[]{:S(2)}, u32[]{:S(2)}) %collective-permute-start.3) | collective-permute-done | bytes 262176 | tf_op jit(solution)/shard_map/ppermute | solution.py:21
  36.0 2.6 %subtract_convert_fusion = bf16[16,2,4096]{2,1,0:T(2,128)(2,1)S(1)} fusion(f32[16,2,4096]{2,1,0:T(2,128)S(1)} %copy-done, f32[16,2,4096]{2,1,0:T(2,128)S(1)} %get-tuple-element.6, f32[16,2,4096]{2,1,0:T(2,128)S(1)} %add.63, f32[16,2,4096]{2,1,0:T(2,128)S(1)} %get-tuple-element.5, f32[16,1,4096]{2,1,0:T(1,128)} %collective-permute-done.3, ...), kind=kLoop, calls=%fused_computation.16 | loop fusion | flops 1835008 | bytes 2916352 | tf_op jit(solution)/shard_map/convert_element_type | solution.py:194
  38.6 0.9 %copy.3 = bf16[2,8,2,4096]{3,1,2,0:T(8,128)(2,1)} copy(bf16[2,8,2,4096]{3,2,1,0:T(2,128)(2,1)S(1)} %bitcast.6) | data formatting | bytes 524288
  39.4 24.3 %shard_map.28 = bf16[16,8192]{1,0:T(8,128)(2,1)} custom-call(bf16[16,8192]{1,0:T(8,128)(2,1)} %bitcast.7), custom_call_target="tpu_custom_call" | custom-call | tf_op jit(solution)/shard_map/pallas_call | solution.py:195
  63.7 1.8 %reshape.32 = bf16[16,2,4096]{2,1,0:T(2,128)(2,1)} reshape(bf16[16,8192]{1,0:T(8,128)(2,1)} %shard_map.28) | data formatting | bytes 524288 | tf_op jit(solution)/shard_map/reshape | solution.py:203
  (3 shorter events, 0.1 us)
Async XLA Ops:
  0.0 7.0 %copy-start = (f32[16,2,4096]{2,1,0:T(2,128)S(1)}, f32[16,2,4096]{2,1,0:T(2,128)}, u32[]{:S(2)}) copy-start(f32[16,2,4096]{2,1,0:T(2,128)} %param.2) | copy-start | bytes 1572868
  1.9 10.1 %collective-permute-start = (f32[16,1,4096]{2,1,0:T(1,128)S(1)}, f32[16,1,4096]{2,1,0:T(1,128)S(1)}, u32[]{:S(2)}, u32[]{:S(2)}) collective-permute-start(f32[16,1,4096]{2,1,0:T(1,128)S(1)} %get-tuple-element.25), channel_id=1, source_target_pairs={{1,0},{2,1},{3,2},{4,3},{5,4},{6,5},{7,6},{0,7},{9,8},{10,9},{11,1... | collective-permute-start | bytes 786440 | tf_op jit(solution)/shard_map/ppermute | solution.py:24
  7.0 9.6 %collective-permute-start.1 = (f32[16,1,4096]{2,1,0:T(1,128)S(1)}, f32[16,1,4096]{2,1,0:T(1,128)S(1)}, u32[]{:S(2)}, u32[]{:S(2)}) collective-permute-start(f32[16,1,4096]{2,1,0:T(1,128)S(1)} %get-tuple-element.26), channel_id=1, source_target_pairs={{0,1},{1,2},{2,3},{3,4},{4,5},{5,6},{6,7},{7,0},{8,9},{9,10},{10,1... | collective-permute-start | bytes 786440 | tf_op jit(solution)/shard_map/ppermute | solution.py:21
  8.4 0.8 %copy-start.1 = (f32[2,4096]{1,0:T(2,128)S(1)}, f32[2,4096]{1,0:T(2,128)}, u32[]{:S(2)}) copy-start(f32[2,4096]{1,0:T(2,128)} %param.3) | copy-start | bytes 98308
  21.0 7.5 %collective-permute-start.2 = (f32[16,1,4096]{2,1,0:T(1,128)}, f32[16,1,4096]{2,1,0:T(1,128)S(1)}, u32[]{:S(2)}, u32[]{:S(2)}) collective-permute-start(f32[16,1,4096]{2,1,0:T(1,128)} %get-tuple-element.23), channel_id=1, source_target_pairs={{1,0},{2,1},{3,2},{4,3},{5,4},{6,5},{7,6},{0,7},{9,8},{10,9},{11,1... | collective-permute-start | bytes 786440 | tf_op jit(solution)/shard_map/ppermute | solution.py:24
  24.2 11.8 %collective-permute-start.3 = (f32[16,1,4096]{2,1,0:T(1,128)}, f32[16,1,4096]{2,1,0:T(1,128)}, u32[]{:S(2)}, u32[]{:S(2)}) collective-permute-start(f32[16,1,4096]{2,1,0:T(1,128)} %get-tuple-element.24), channel_id=1, source_target_pairs={{0,1},{1,2},{2,3},{3,4},{4,5},{5,6},{6,7},{7,0},{8,9},{9,10},{10,1... | collective-permute-start | bytes 786440 | tf_op jit(solution)/shard_map/ppermute | solution.py:21

commit v2 on v1

v2 whole, which is shorter than its diff:
```python
import functools

import jax
import jax.numpy as jnp
from jax import lax
from jax.experimental import pallas as pl
from jax.experimental.pallas import tpu as pltpu
from jax.sharding import PartitionSpec as P

NS_ITERS = 2
LANES = 128
HALF = LANES // 2


def remote(src, dst, send, recv, **where):
    return pltpu.make_async_remote_copy(
        src_ref=src, dst_ref=dst, send_sem=send, recv_sem=recv,
        device_id=where, device_id_type=pl.DeviceIdType.MESH,
    )


def newton_schulz(gram):
    size = gram.shape[0]
    scale = jnp.max(jnp.sum(jnp.abs(gram), axis=1, keepdims=True), axis=0, keepdims=True)
    rows = lax.broadcasted_iota(jnp.int32, (size, size), 0)
    cols = lax.broadcasted_iota(jnp.int32, (size, size), 1)
    identity_mat = (rows == cols).astype(jnp.float32)
    upper = gram / scale
    lower = None
    for sweep in range(NS_ITERS):
        product = upper if lower is None else jnp.dot(
            lower, upper, precision=lax.Precision.HIGHEST, preferred_element_type=jnp.float32)
        factor = 1.5 * identity_mat - 0.5 * product
        if sweep < NS_ITERS - 1:
            upper = jnp.dot(upper, factor, precision=lax.Precision.HIGHEST,
                            preferred_element_type=jnp.float32)
        lower = factor if lower is None else jnp.dot(
            factor, lower, precision=lax.Precision.HIGHEST, preferred_element_type=jnp.float32)
    return lower / jnp.sqrt(scale)


def exchange(n, axis, me, src_of, dst_of, send, recv):
    sends = []
    for step in range(1, n):
        peer = lax.rem(me + step, n)
        copy = remote(src_of(peer), dst_of(me), send.at[step], recv.at[step], **{axis: peer})
        copy.start()
        sends.append(copy)

    def arrived():
        for step in range(1, n):
            source = lax.rem(me + n - step, n)
            remote(src_of(source), dst_of(source), send.at[step], recv.at[step],
                   **{axis: source}).wait_recv()

    def sent():
        for copy in sends:
            copy.wait_send()

    return arrived, sent


def rows_of(index, size):
    return pl.ds(pl.multiple_of(index * size, size), size)


def sideways(block, lane, before, after):
    turned = pltpu.roll(block, HALF, 1)
    inner = lane % HALF
    below = pltpu.roll(jnp.where(inner == HALF - 1, turned, block), 1, 1)
    above = pltpu.roll(jnp.where(inner == 0, turned, block), LANES - 1, 1)
    rows = turned + pltpu.roll(jnp.where(lane >= HALF, before, after), HALF, 1)
    return rows + (below + above)


def filter_planes(width, pot, slab, first, filt, firsts, seconds):
    blocks = width // LANES

    def columns(index):
        return pl.ds(pl.multiple_of(index * LANES, LANES), LANES)

    def at(plane):
        return slab.at[plane // 2, plane % 2]

    lane = lax.broadcasted_iota(jnp.int32, (slab.shape[2], LANES), 1)

    def places(index):
        return (columns(index), columns(lax.rem(index + blocks - 1, blocks)),
                columns(lax.rem(index + 1, blocks)))

    def level(plane, here):
        return (pot[plane // 2, pl.ds(plane % 2, 1), here] - 2.0) * (1.0 / 3.0)

    def step1(index, carry):
        here, before, after = places(index)
        for plane in firsts:
            ref = at(plane)
            beside = sideways(ref[:, here], lane, ref[:, before], ref[:, after])
            beside = beside + (at(plane - 1)[:, here] + at(plane + 1)[:, here])
            first[plane, :, here] = level(plane, here) * ref[:, here] - beside * (1.0 / 6.0)
        return carry

    def step2(index, carry):
        here, before, after = places(index)
        for plane in seconds:
            ref = first.at[plane]
            beside = sideways(ref[:, here], lane, ref[:, before], ref[:, after])
            beside = beside + (first[plane - 1, :, here] + first[plane + 1, :, here])
            value = 2.0 * level(plane, here) * ref[:, here] - beside * (1.0 / 3.0)
            filt[plane - 2, :, here] = (value - at(plane)[:, here]).astype(jnp.bfloat16)
        return carry

    if firsts:
        lax.fori_loop(0, blocks, step1, 0, unroll=2)
    if seconds:
        lax.fori_loop(0, blocks, step2, 0, unroll=2)


def kernel(nb, ng, orb_ref, pot_ref, out_ref, slab, pot, first, filt, parts,
           pieces, turned, gpart, rs, gr, gfull, own_sem, hs, hr, ps, pr, fs, fr,
           s1, r1, s2, r2, s3, r3, s4, r4):
    count, width = orb_ref.shape[1:]
    half = count // 2
    orbs = nb * count
    share = pieces.shape[1]
    per_plane = nb // 2
    pairs = ng // 2
    total_cells = share * nb * ng
    b = lax.axis_index("band")
    g = lax.axis_index("grid")
    pair = g // 2
    h = g % 2
    other = 1 - h
    partner = 2 * pair + other
    low = 2 * lax.rem(pair + pairs - 1, pairs)
    high = 2 * lax.rem(pair + 1, pairs)
    target = 2 * lax.rem(pair + pairs - 1 + 2 * h, pairs)
    slot = 3 - 3 * h

    barrier = pltpu.get_barrier_semaphore()
    for step in range(1, ng):
        pl.semaphore_signal(barrier, inc=1, device_id={"grid": lax.rem(g + step, ng)},
                            device_id_type=pl.DeviceIdType.MESH)
    for step in range(1, nb):
        for where in (g, partner):
            pl.semaphore_signal(
                barrier, inc=1, device_id={"band": lax.rem(b + step, nb), "grid": where},
                device_id_type=pl.DeviceIdType.MESH)

    def orbital_rows(index):
        return orb_ref.at[:, rows_of(index, half)]

    own = [pltpu.make_async_copy(orbital_rows(h), slab.at[1 + h], own_sem.at[0]),
           pltpu.make_async_copy(pot_ref, pot.at[1 + h], own_sem.at[1])]
    for copy in own:
        copy.start()
    pl.semaphore_wait(barrier, ng - 1 + 2 * (nb - 1))

    def across(index, where, to_slot, send):
        return [
            remote(orbital_rows(index), slab.at[to_slot], hs.at[send], hr.at[to_slot], grid=where),
            remote(pot_ref, pot.at[to_slot], ps.at[send], pr.at[to_slot], grid=where)]

    moves = (across(h, target + h, slot, 0) + across(other, partner, 1 + h, 1)
             + across(other, target + other, slot, 2))
    for copy in moves:
        copy.start()

    def landed(source, from_slot):
        for copy in across(h, source, from_slot, 0):
            copy.wait_recv()

    for copy in own:
        copy.wait()
    landed(partner, 2 - h)
    filter_planes(width, pot, slab, first, filt, (3, 4), ())
    landed(low + 1, 0)
    filter_planes(width, pot, slab, first, filt, (1, 2), (2, 3))
    landed(high, 3)
    filter_planes(width, pot, slab, first, filt, (5, 6), (4, 5))

    def cells_for(to_h, to_b):
        return filt.at[2 * to_h + to_b // per_plane, :,
                       rows_of(to_b % per_plane, share)]

    mine = pltpu.make_async_copy(cells_for(h, b), parts.at[b, h], own_sem.at[2])
    mine.start()
    spread = []
    for dh in (1, 0):
        for db in range(nb):
            if dh + db:
                to_h = (h + dh) % 2
                to_b = lax.rem(b + db, nb)
                copy = remote(cells_for(to_h, to_b), parts.at[b, h], fs.at[dh * nb + db],
                              fr.at[dh * nb + db], band=to_b, grid=2 * pair + to_h)
                copy.start()
                spread.append(copy)
    gpart[...] = jnp.zeros_like(gpart)
    mine.wait()
    for dh in (0, 1):
        for db in range(nb):
            if dh + db:
                from_h = (h + dh) % 2
                from_b = lax.rem(b + nb - db, nb)
                remote(cells_for(from_h, from_b), parts.at[from_b, from_h], fs.at[dh * nb + db],
                       fr.at[dh * nb + db], band=from_b, grid=2 * pair + from_h).wait_recv()
    for index in range(nb):
        both = jnp.concatenate([parts[index, 0].astype(jnp.float32),
                                parts[index, 1].astype(jnp.float32)], axis=0)
        pieces[index * count:(index + 1) * count, :] = both.astype(jnp.bfloat16)
    everything = pieces[...]
    gpart[:, :orbs] = lax.dot_general(
        everything, everything, (((1,), (1,)), ((), ())),
        preferred_element_type=jnp.float32) / total_cells
    arrived1, sent1 = exchange(
        nb, "band", b, lambda p: gpart.at[rows_of(p, count)], lambda p: rs.at[p], s1, r1)
    rs[b] = gpart[rows_of(b, count), :]
    arrived1()
    gr[g] = jnp.sum(rs[...], axis=0)
    arrived2, sent2 = exchange(ng, "grid", g, lambda p: gr.at[g], lambda p: gr.at[p], s2, r2)
    arrived2()
    gfull[rows_of(b, count), :] = jnp.sum(gr[...], axis=0)
    arrived3, sent3 = exchange(
        nb, "band", b, lambda p: gfull.at[rows_of(b, count)],
        lambda p: gfull.at[rows_of(p, count)], s3, r3)
    arrived3()
    root = newton_schulz(gfull[:, :orbs]).astype(jnp.bfloat16)
    turned[...] = lax.dot_general(
        root, pieces[...], (((0,), (0,)), ((), ())),
        preferred_element_type=jnp.float32).astype(jnp.bfloat16)
    back = pltpu.make_async_copy(
        turned.at[rows_of(b, count)], out_ref.at[:, rows_of(b, share)], own_sem.at[3])
    back.start()
    arrived4, sent4 = exchange(
        nb, "band", b, lambda p: turned.at[rows_of(p, count)],
        lambda p: out_ref.at[:, rows_of(p, share)], s4, r4)
    arrived4()
    back.wait()
    for copy in moves + spread:
        copy.wait_send()
    for done in (sent1, sent2, sent3, sent4):
        done()


def local(orbitals, potential):
    count, zplanes, width = orbitals.shape
    cells = zplanes * width
    nb = lax.axis_size("band")
    ng = lax.axis_size("grid")
    half = count // 2
    orbs = nb * count
    wide = max(LANES, orbs)
    share = cells // nb
    bf16, f32 = jnp.bfloat16, jnp.float32
    dma = pltpu.SemaphoreType.DMA
    returned = pl.pallas_call(
        functools.partial(kernel, nb, ng),
        out_shape=jax.ShapeDtypeStruct((count, cells), bf16),
        in_specs=[pl.BlockSpec(memory_space=pltpu.VMEM)] * 2,
        out_specs=pl.BlockSpec(memory_space=pltpu.VMEM),
        scratch_shapes=[
            pltpu.VMEM((4, zplanes, half, width), f32),
            pltpu.VMEM((4, zplanes, width), f32),
            pltpu.VMEM((8, half, width), f32),
            pltpu.VMEM((4, half, width), bf16),
            pltpu.VMEM((nb, 2, half, share), bf16),
            pltpu.VMEM((orbs, share), bf16),
            pltpu.VMEM((orbs, share), bf16),
            pltpu.VMEM((orbs, wide), f32),
            pltpu.VMEM((nb, count, wide), f32),
            pltpu.VMEM((ng, count, wide), f32),
            pltpu.VMEM((orbs, wide), f32),
            dma((4,)), dma((3,)), dma((4,)), dma((3,)), dma((4,)), dma((2 * nb,)), dma((2 * nb,)),
            dma((nb,)), dma((nb,)), dma((ng,)), dma((ng,)),
            dma((nb,)), dma((nb,)), dma((nb,)), dma((nb,)),
        ],
        compiler_params=pltpu.CompilerParams(collective_id=0, has_side_effects=True),
    )(jnp.swapaxes(orbitals, 0, 1), potential)
    return returned.reshape(count, zplanes, width)


def solution(mesh):
    placed = (P("band", "grid", None), P("grid", None))
    return jax.shard_map(
        local, mesh=mesh, in_specs=placed, out_specs=P("band", "grid", None), check_vma=False
    )
```

time: 65.8 us -> 57.2 us (0.87)
  Pallas kernels: 24.3 us -> 53 us
  waiting for transfers between devices: 16.4 us -> 0 us
  starting transfers between devices: 8.3 us -> 0 us
  local copies, waits for them, and re-layouts: 10.7 us -> 3.98 us
  other arithmetic: 5.81 us -> 0 us
    pallas_call x1, Pallas kernels: 24.3 us -> 53 us  [local(): pl.pallas_call(functools.partial(kernel, nb, ng), out_shape=jax.ShapeDtyp...]
    ppermute x4 -> x0, waiting for transfers between devices: 16.4 us -> none  [the longest x2 12 us: with_halo(): lax.ppermute(lax.slice_in_dim(block, block.shape[dim] - width, None, axis...]
    ppermute x4 -> x0, starting transfers between devices: 8.3 us -> none  [the longest x2 8.29 us: with_halo(): lax.ppermute(lax.slice_in_dim(block, 0, width, axis=dim), axis, backward)]
    slice x10 -> x0, local copies, waits for them, and re-layouts: 5.13 us -> none  [the longest x2 3.22 us: with_halo(): lax.slice_in_dim(block, 0, width, axis=dim)]
    convert_element_type x1 -> x0, other arithmetic: 2.58 us -> none  [local(): filtered = current.astype(jnp.bfloat16).reshape(count, cells)]
    add x2 -> x0, other arithmetic: 1.72 us -> none  [apply_inner(): sideways = sideways + jnp.roll(square, 1, 3) + jnp.roll(square, -1, 3)]
    div x1 -> x0, other arithmetic: 1.49 us -> none  [local(): following = (applied - 5.0 * current) / 3.0]
    reshape x2 -> x0, local copies, waits for them, and re-layouts: 1.24 us -> none  [apply_inner(): square = inner.reshape(count, planes, NX, NX)]
  transfers between devices with their start and end apart: 4 -> 0, of which waited for: 4 -> 0; matrix products, arithmetic and copies ran while one was open for 7% -> 0% of each run, Pallas kernels for 0% -> 0%
where the time goes in v2:
time: 57.2 us; the launch traced here: 57 us
  Pallas kernels  53 us (93%)
  local copies, waits for them, and re-layouts  3.98 us (7%)
    pallas_call x1, Pallas kernels, local(): pl.pallas_call(functools.partial(kernel, nb, ng), out_shape=jax.ShapeDtyp...  53 us
    unnamed x1, local copies, waits for them, and re-layouts  2.14 us
    reshape x1, local copies, waits for them, and re-layouts, local(): return returned.reshape(count, zplanes, width)  1.85 us

profile of v2, /device:TPU:1, one launch (start us, length us, event | category | flops | bytes accessed | tf_op | source)
XLA Modules:
  0.0 57.0 jit_solution(12137662559887933339)
XLA Ops:
  0.0 2.1 %copy.5 = f32[16,2,4096]{2,0,1:T(8,128)} copy(f32[16,2,4096]{2,1,0:T(2,128)} %param.2) | data formatting | bytes 1048576 | tf_op args[0]
  2.1 53.0 %shard_map.28 = bf16[16,8192]{1,0:T(8,128)(2,1)} custom-call(f32[2,16,4096]{2,1,0:T(8,128)} %bitcast.3, f32[2,4096]{1,0:T(2,128)} %pot_ref.1), custom_call_target="tpu_custom_call" | custom-call | tf_op jit(solution)/shard_map/pallas_call | solution.py:256
  55.2 1.8 %reshape.3 = bf16[16,2,4096]{2,1,0:T(2,128)(2,1)} reshape(bf16[16,8192]{1,0:T(8,128)(2,1)} %shard_map.28) | data formatting | bytes 524288 | tf_op jit(solution)/shard_map/reshape | solution.py:279

commit v3 on v2

--- a/solution.py
+++ b/solution.py
@@ -111,16 +111,17 @@
         return carry
 
     if firsts:
-        lax.fori_loop(0, blocks, step1, 0, unroll=2)
+        lax.fori_loop(0, blocks, step1, 0, unroll=16)
     if seconds:
-        lax.fori_loop(0, blocks, step2, 0, unroll=2)
-
-
-def kernel(nb, ng, orb_ref, pot_ref, out_ref, slab, pot, first, filt, parts,
-           pieces, turned, gpart, rs, gr, gfull, own_sem, hs, hr, ps, pr, fs, fr,
+        lax.fori_loop(0, blocks, step2, 0, unroll=16)
+
+
+def kernel(nb, ng, orb_ref, pot_ref, out_ref, raw, slab, pot, first, filt, parts,
+           pieces, turned, gpart, rs, gr, gfull, landing, spaced, own_sem, hs, hr, ps, pr, fs, fr,
            s1, r1, s2, r2, s3, r3, s4, r4):
-    count, width = orb_ref.shape[1:]
-    half = count // 2
+    half, width = slab.shape[2:]
+    count = 2 * half
+    deep = 2 * width // LANES
     orbs = nb * count
     share = pieces.shape[1]
     per_plane = nb // 2
@@ -148,9 +149,9 @@
                 device_id_type=pl.DeviceIdType.MESH)
 
     def orbital_rows(index):
-        return orb_ref.at[:, rows_of(index, half)]
-
-    own = [pltpu.make_async_copy(orbital_rows(h), slab.at[1 + h], own_sem.at[0]),
+        return orb_ref.at[rows_of(index, half * deep)]
+
+    own = [pltpu.make_async_copy(orbital_rows(h), raw.at[1 + h], own_sem.at[0]),
            pltpu.make_async_copy(pot_ref, pot.at[1 + h], own_sem.at[1])]
     for copy in own:
         copy.start()
@@ -158,7 +159,7 @@
 
     def across(index, where, to_slot, send):
         return [
-            remote(orbital_rows(index), slab.at[to_slot], hs.at[send], hr.at[to_slot], grid=where),
+            remote(orbital_rows(index), raw.at[to_slot], hs.at[send], hr.at[to_slot], grid=where),
             remote(pot_ref, pot.at[to_slot], ps.at[send], pr.at[to_slot], grid=where)]
 
     moves = (across(h, target + h, slot, 0) + across(other, partner, 1 + h, 1)
@@ -166,17 +167,31 @@
     for copy in moves:
         copy.start()
 
+    def unpack(at_slot):
+        def column(index, carry):
+            where = pl.ds(pl.multiple_of(index * LANES, LANES), LANES)
+            for plane in range(2):
+                slab[at_slot, plane, :, where] = raw[
+                    at_slot, pl.ds(2 * index + plane, half, stride=deep), :]
+            return carry
+
+        lax.fori_loop(0, width // LANES, column, 0, unroll=8)
+
     def landed(source, from_slot):
         for copy in across(h, source, from_slot, 0):
             copy.wait_recv()
 
     for copy in own:
         copy.wait()
+    unpack(1 + h)
     landed(partner, 2 - h)
+    unpack(2 - h)
     filter_planes(width, pot, slab, first, filt, (3, 4), ())
     landed(low + 1, 0)
+    unpack(0)
     filter_planes(width, pot, slab, first, filt, (1, 2), (2, 3))
     landed(high, 3)
+    unpack(3)
     filter_planes(width, pot, slab, first, filt, (5, 6), (4, 5))
 
     def cells_for(to_h, to_b):
@@ -228,14 +243,25 @@
     turned[...] = lax.dot_general(
         root, pieces[...], (((0,), (0,)), ((), ())),
         preferred_element_type=jnp.float32).astype(jnp.bfloat16)
-    back = pltpu.make_async_copy(
-        turned.at[rows_of(b, count)], out_ref.at[:, rows_of(b, share)], own_sem.at[3])
-    back.start()
     arrived4, sent4 = exchange(
-        nb, "band", b, lambda p: turned.at[rows_of(p, count)],
-        lambda p: out_ref.at[:, rows_of(p, share)], s4, r4)
-    arrived4()
-    back.wait()
+        nb, "band", b, lambda p: turned.at[rows_of(p, count)], lambda p: landing.at[p], s4, r4)
+
+    def place(owner, block):
+        blocks = share // LANES
+        base = 2 * blocks * (owner % per_plane) + owner // per_plane
+        for index in range(blocks):
+            values = block[:, index * LANES:(index + 1) * LANES].astype(jnp.float32)
+            for part in range(2):
+                spaced[pl.ds(part * half * deep + base + 2 * index, half, stride=deep), :] = (
+                    values[part * half:(part + 1) * half])
+
+    place(b, turned[rows_of(b, count), :])
+    for step in range(1, nb):
+        source = lax.rem(b + nb - step, nb)
+        remote(turned.at[rows_of(source, count)], landing.at[source], s4.at[step], r4.at[step],
+               band=source).wait_recv()
+        place(source, landing[source])
+    out_ref[...] = spaced[...].astype(jnp.bfloat16)
     for copy in moves + spread:
         copy.wait_send()
     for done in (sent1, sent2, sent3, sent4):
@@ -255,10 +281,11 @@
     dma = pltpu.SemaphoreType.DMA
     returned = pl.pallas_call(
         functools.partial(kernel, nb, ng),
-        out_shape=jax.ShapeDtypeStruct((count, cells), bf16),
-        in_specs=[pl.BlockSpec(memory_space=pltpu.VMEM)] * 2,
+        out_shape=jax.ShapeDtypeStruct((count * cells // LANES, LANES), bf16),
+        in_specs=[pl.BlockSpec(memory_space=pl.ANY)] * 2,
         out_specs=pl.BlockSpec(memory_space=pltpu.VMEM),
         scratch_shapes=[
+            pltpu.VMEM((4, half * cells // LANES, LANES), f32),
             pltpu.VMEM((4, zplanes, half, width), f32),
             pltpu.VMEM((4, zplanes, width), f32),
             pltpu.VMEM((8, half, width), f32),
@@ -270,13 +297,17 @@
             pltpu.VMEM((nb, count, wide), f32),
             pltpu.VMEM((ng, count, wide), f32),
             pltpu.VMEM((orbs, wide), f32),
+            pltpu.VMEM((nb, count, share), bf16),
+            pltpu.VMEM((count * cells // LANES, LANES), f32),
             dma((4,)), dma((3,)), dma((4,)), dma((3,)), dma((4,)), dma((2 * nb,)), dma((2 * nb,)),
             dma((nb,)), dma((nb,)), dma((ng,)), dma((ng,)),
             dma((nb,)), dma((nb,)), dma((nb,)), dma((nb,)),
         ],
         compiler_params=pltpu.CompilerParams(collective_id=0, has_side_effects=True),
-    )(jnp.swapaxes(orbitals, 0, 1), potential)
-    return returned.reshape(count, zplanes, width)
+    )(orbitals.reshape(count, zplanes, width // LANES, LANES).swapaxes(1, 2).reshape(-1, LANES),
+      potential)
+    spread = returned.reshape(count, width // LANES, zplanes, LANES).swapaxes(1, 2)
+    return spread.reshape(count, zplanes, width)
 
 
 def solution(mesh):

time: 57.2 us -> 45.3 us (0.79)
  Pallas kernels: 53 us -> 43.3 us
  local copies, waits for them, and re-layouts: 3.98 us -> 1.85 us
    pallas_call x1, Pallas kernels: 53 us -> 43.3 us  [local(): pl.pallas_call(functools.partial(kernel, nb, ng), out_shape=jax.ShapeDtyp...]
    reshape x1 -> x0, local copies, waits for them, and re-layouts: 1.85 us -> none  [local(): return returned.reshape(count, zplanes, width)]
where the time goes in v3:
time: 45.3 us; the launch traced here: 45.1 us
  Pallas kernels  43.3 us (96%)
  local copies, waits for them, and re-layouts  1.85 us (4%)
    pallas_call x1, Pallas kernels, local(): pl.pallas_call(functools.partial(kernel, nb, ng), out_shape=jax.ShapeDtyp...  43.3 us
    unnamed x1, local copies, waits for them, and re-layouts  1.85 us

profile of v3, /device:TPU:1, one launch (start us, length us, event | category | flops | bytes accessed | tf_op | source)
XLA Modules:
  0.0 45.1 jit_solution(9701019277692104867)
XLA Ops:
  0.0 43.3 %shard_map.28 = bf16[1024,128]{1,0:T(8,128)(2,1)} custom-call(f32[1024,128]{1,0:T(8,128)} %bitcast.11, f32[2,4096]{1,0:T(2,128)} %pot_ref.1), custom_call_target="tpu_custom_call" | custom-call | tf_op jit(solution)/shard_map/pallas_call | solution.py:282
  43.3 1.9 %copy.6 = bf16[16,2,4096]{2,1,0:T(2,128)(2,1)} copy(bf16[16,2,4096]{2,1,0:T(2,128)(2,1)} %bitcast.10) | data formatting | bytes 524288

commit v4 on v3

--- a/solution.py
+++ b/solution.py
@@ -210,7 +210,6 @@
                               fr.at[dh * nb + db], band=to_b, grid=2 * pair + to_h)
                 copy.start()
                 spread.append(copy)
-    gpart[...] = jnp.zeros_like(gpart)
     mine.wait()
     for dh in (0, 1):
         for db in range(nb):
@@ -224,22 +223,30 @@
                                 parts[index, 1].astype(jnp.float32)], axis=0)
         pieces[index * count:(index + 1) * count, :] = both.astype(jnp.bfloat16)
     everything = pieces[...]
-    gpart[:, :orbs] = lax.dot_general(
+    gram = lax.dot_general(
         everything, everything, (((1,), (1,)), ((), ())),
         preferred_element_type=jnp.float32) / total_cells
+    rows = gpart.shape[1]
+    fold = count // rows
+    for index in range(nb):
+        for part in range(fold):
+            start = index * count + part * rows
+            gpart[index, :, part * orbs:(part + 1) * orbs] = gram[start:start + rows]
     arrived1, sent1 = exchange(
-        nb, "band", b, lambda p: gpart.at[rows_of(p, count)], lambda p: rs.at[p], s1, r1)
-    rs[b] = gpart[rows_of(b, count), :]
+        nb, "band", b, lambda p: gpart.at[p], lambda p: rs.at[p], s1, r1)
+    rs[b] = gpart[b]
     arrived1()
     gr[g] = jnp.sum(rs[...], axis=0)
     arrived2, sent2 = exchange(ng, "grid", g, lambda p: gr.at[g], lambda p: gr.at[p], s2, r2)
     arrived2()
-    gfull[rows_of(b, count), :] = jnp.sum(gr[...], axis=0)
+    gfull[b] = jnp.sum(gr[...], axis=0)
     arrived3, sent3 = exchange(
-        nb, "band", b, lambda p: gfull.at[rows_of(b, count)],
-        lambda p: gfull.at[rows_of(p, count)], s3, r3)
+        nb, "band", b, lambda p: gfull.at[b], lambda p: gfull.at[p], s3, r3)
     arrived3()
-    root = newton_schulz(gfull[:, :orbs]).astype(jnp.bfloat16)
+    gram = jnp.concatenate(
+        [gfull[index, :, part * orbs:(part + 1) * orbs]
+         for index in range(nb) for part in range(fold)], axis=0)
+    root = newton_schulz(gram).astype(jnp.bfloat16)
     turned[...] = lax.dot_general(
         root, pieces[...], (((0,), (0,)), ((), ())),
         preferred_element_type=jnp.float32).astype(jnp.bfloat16)
@@ -275,7 +282,9 @@
     ng = lax.axis_size("grid")
     half = count // 2
     orbs = nb * count
-    wide = max(LANES, orbs)
+    fold = 2 if 2 * orbs == LANES else 1
+    wide = fold * orbs
+    packed = count // fold
     share = cells // nb
     bf16, f32 = jnp.bfloat16, jnp.float32
     dma = pltpu.SemaphoreType.DMA
@@ -293,17 +302,18 @@
             pltpu.VMEM((nb, 2, half, share), bf16),
             pltpu.VMEM((orbs, share), bf16),
             pltpu.VMEM((orbs, share), bf16),
-            pltpu.VMEM((orbs, wide), f32),
-            pltpu.VMEM((nb, count, wide), f32),
-            pltpu.VMEM((ng, count, wide), f32),
-            pltpu.VMEM((orbs, wide), f32),
+            pltpu.VMEM((nb, packed, wide), f32),
+            pltpu.VMEM((nb, packed, wide), f32),
+            pltpu.VMEM((ng, packed, wide), f32),
+            pltpu.VMEM((nb, packed, wide), f32),
             pltpu.VMEM((nb, count, share), bf16),
             pltpu.VMEM((count * cells // LANES, LANES), f32),
             dma((4,)), dma((3,)), dma((4,)), dma((3,)), dma((4,)), dma((2 * nb,)), dma((2 * nb,)),
             dma((nb,)), dma((nb,)), dma((ng,)), dma((ng,)),
             dma((nb,)), dma((nb,)), dma((nb,)), dma((nb,)),
         ],
-        compiler_params=pltpu.CompilerParams(collective_id=0, has_side_effects=True),
+        compiler_params=pltpu.CompilerParams(collective_id=0, has_side_effects=True,
+                                             vmem_limit_bytes=16 * 2**20),
     )(orbitals.reshape(count, zplanes, width // LANES, LANES).swapaxes(1, 2).reshape(-1, LANES),
       potential)
     spread = returned.reshape(count, width // LANES, zplanes, LANES).swapaxes(1, 2)

time: 45.3 us -> 45.1 us (level)
  Pallas kernels: 43.3 us -> 42.3 us
  local copies, waits for them, and re-layouts: 1.85 us -> 2.5 us
    pallas_call x1, Pallas kernels: 43.3 us -> 42.3 us  [local(): pl.pallas_call(functools.partial(kernel, nb, ng), out_shape=jax.ShapeDtyp...]
    unnamed x1 -> x5, local copies, waits for them, and re-layouts: 1.85 us -> 2.5 us
where the time goes in v4:
time: 45.1 us; the launch traced here: 44.9 us
  Pallas kernels  42.3 us (94%)
  local copies, waits for them, and re-layouts  2.5 us (6%)
    pallas_call x1, Pallas kernels, local(): pl.pallas_call(functools.partial(kernel, nb, ng), out_shape=jax.ShapeDtyp...  42.3 us
    unnamed x5, local copies, waits for them, and re-layouts  2.5 us

profile of v4, /device:TPU:1, one launch (start us, length us, event | category | flops | bytes accessed | tf_op | source)
XLA Modules:
  0.0 44.9 jit_solution(15003992521313773557)
XLA Ops:
  0.0 0.0 copy-start
  0.0 1.0 %copy-done = f32[16,2,4096]{2,1,0:T(2,128)S(1)} copy-done((f32[16,2,4096]{2,1,0:T(2,128)S(1)}, f32[16,2,4096]{2,1,0:T(2,128)}, u32[]{:S(2)}) %copy-start) | copy-done | bytes 524312
  1.0 0.0 copy-start.1
  1.0 0.8 %copy-done.1 = f32[2,4096]{1,0:T(2,128)S(1)} copy-done((f32[2,4096]{1,0:T(2,128)S(1)}, f32[2,4096]{1,0:T(2,128)}, u32[]{:S(2)}) %copy-start.1) | copy-done | bytes 32792
  1.8 42.3 %shard_map.28 = bf16[1024,128]{1,0:T(8,128)(2,1)S(1)} custom-call(f32[1024,128]{1,0:T(8,128)S(1)} %bitcast.11, f32[2,4096]{1,0:T(2,128)S(1)} %copy-done.1), custom_call_target="tpu_custom_call" | custom-call | tf_op jit(solution)/shard_map/pallas_call | solution.py:291
  44.2 0.7 %copy.6 = bf16[16,2,4096]{2,1,0:T(2,128)(2,1)} copy(bf16[16,2,4096]{2,1,0:T(2,128)(2,1)S(1)} %bitcast.10) | data formatting | bytes 524288
Async XLA Ops:
  0.0 1.0 %copy-start = (f32[16,2,4096]{2,1,0:T(2,128)S(1)}, f32[16,2,4096]{2,1,0:T(2,128)}, u32[]{:S(2)}) copy-start(f32[16,2,4096]{2,1,0:T(2,128)} %param.2) | copy-start | bytes 1572868
  1.0 0.8 %copy-start.1 = (f32[2,4096]{1,0:T(2,128)S(1)}, f32[2,4096]{1,0:T(2,128)}, u32[]{:S(2)}) copy-start(f32[2,4096]{1,0:T(2,128)} %pot_ref.1) | copy-start | bytes 98308
